TPU v7x, 768 devices: a whole 4x8x12 slice. The times are simulated.
768 devices in a mesh: gx: 16 (over y_lo, x), gy: 48 (over y_hi, z, core).
Axes of the slice: x: 4, y: 8 (y_hi: 2, y_lo: 4; y = y_hi * 4 + y_lo), z: 12, core: 2. Of those that a mesh axis runs over, the one named last changes fastest.
Arguments:
- positions: bfloat16 [16, 48, 3, 128], P('gx', 'gy'), may hold values from -0.5 to 0.5
- features: bfloat16 [16, 48, 128, 128], P('gx', 'gy'), may hold values from -6 to 6
- senders: int32 [16, 48, 1, 8], P('gx', 'gy'), may hold values from 0 to 8, as said below
- counts: int32 [16, 48, 1], P('gx', 'gy'), may hold values from 1 to 5, as said below
- radial_w: float32 [2, 8, 128], replicated, may hold values from -0.36 to 0.36
- mix_w: bfloat16 [128, 128], replicated, may hold values from -0.5 to 0.5
- square_w: bfloat16 [128, 128], replicated, may hold values from -0.5 to 0.5
- cotangent: bfloat16 [16, 48, 128, 128], P('gx', 'gy'), may hold values from -6 to 6
Outputs:
- updated: bfloat16 [16, 48, 128, 128], P('gx', 'gy')
- grad_features: float32 [16, 48, 128, 128], P('gx', 'gy')
Inputs may be any that keep to these rules, and one draw needn't show every extreme that they name: `senders`: an entry g names ghost block g of the receiver's cell (see the steps); the 8 entries of one receiver block differ. Over the 1 receiver blocks of one cell the counts sum to at most 5, and some cell reaches 5 in every draw.
All inputs are finite; a program needn't handle non-finite values.
Results may differ from a plain program's by a relative error of at most 0.005.
The roundings to bfloat16 on the way count: a program that leaves them out, or rounds other values in their place, can miss the bound.
Values may be sent and summed in bfloat16 or wider, within the bound.
A program may use at most 32 MiB of HBM per device.

v0:
```python
import functools
import math

import jax
import jax.numpy as jnp
from jax import lax
from jax.experimental import pallas as pl
from jax.experimental.pallas import tpu as pltpu
from jax.sharding import PartitionSpec as P

MESH = pl.DeviceIdType.MESH
BLK = 128
CH = 128
NRAD = 8
GHOSTS = 9
OWN = 4
F32 = jnp.float32
BF16 = jnp.bfloat16

SERIES = [(-1.0) ** (n + 1) * math.pi ** (2 * n + 1) / math.factorial(2 * n + 1) for n in range(7)]


def radial(dx, dy, dz, keep):
    dist = jnp.sqrt(dx * dx + dy * dy + dz * dz)
    u = jnp.minimum(dist, 1.0)
    one_minus = 1.0 - u
    value = one_minus * one_minus * keep
    v = u - 0.5
    v2 = v * v
    acc = jnp.full_like(v2, SERIES[6])
    for coef in SERIES[5::-1]:
        acc = acc * v2 + coef
    cosine = acc * v
    twice = cosine + cosine
    out = [value, value * cosine]
    for _ in range(NRAD - 2):
        out.append(twice * out[-1] - out[-2])
    return [b.astype(BF16) for b in out]


def columns(rows):
    padded = jnp.concatenate([rows, jnp.zeros((BLK - 3, BLK), F32)], axis=0)
    return padded.T


def kernel(
    nx, ny,
    pos_ref, feat_ref, senders_ref, counts_ref, rad_ref, mix_ref, square_ref, cot_ref,
    updated_ref, grad_ref,
    gpos, gfeat, basis, basis_t, stack, gbasis, gcols, out_grad, in_grad,
    psend, precv, fsend, frecv, gsend, grecv,
):
    gx = lax.axis_index("gx")
    gy = lax.axis_index("gy")

    def peer(g):
        return (lax.rem(gx + (g // 3 - 1) + nx, nx), lax.rem(gy + (g % 3 - 1) + ny, ny))

    others = [g for g in range(GHOSTS) if g != OWN]
    barrier = pltpu.get_barrier_semaphore()
    for g in others:
        pl.semaphore_signal(barrier, inc=1, device_id=peer(g), device_id_type=MESH)
    pl.semaphore_wait(barrier, len(others))

    def pos_copy(g):
        return pltpu.make_async_remote_copy(
            src_ref=pos_ref.at[0, 0], dst_ref=gpos.at[8 - g], send_sem=psend.at[g],
            recv_sem=precv.at[8 - g], device_id=peer(g), device_id_type=MESH)

    def feat_copy(g):
        return pltpu.make_async_remote_copy(
            src_ref=feat_ref.at[0, 0], dst_ref=gfeat.at[8 - g], send_sem=fsend.at[g],
            recv_sem=frecv.at[8 - g], device_id=peer(g), device_id_type=MESH)

    def grad_copy(g):
        return pltpu.make_async_remote_copy(
            src_ref=out_grad.at[g], dst_ref=in_grad.at[8 - g], send_sem=gsend.at[g],
            recv_sem=grecv.at[8 - g], device_id=peer(g), device_id_type=MESH)

    for g in others:
        pos_copy(g).start()
    for g in others:
        feat_copy(g).start()

    own_rows = pos_ref[0, 0].astype(F32)
    own_cols = columns(own_rows)
    own_x = [own_rows[m:m + 1, :] for m in range(3)]
    own_c = [own_cols[:, m:m + 1] for m in range(3)]
    count = counts_ref[0, 0, 0]
    cot = cot_ref[0, 0]
    nt = (((1,), (1,)), ((), ()))
    grad_first = lax.dot_general(cot, mix_ref[...], nt, preferred_element_type=F32)
    diagonal = lax.broadcasted_iota(jnp.int32, (BLK, BLK), 0) == lax.broadcasted_iota(jnp.int32, (BLK, BLK), 1)

    def tile(p, own):
        g = lax.rem(p + OWN, GHOSTS)
        live = jnp.int32(0)
        for t in range(8):
            live = live + jnp.where((senders_ref[0, 0, 0, t] == g) & (t < count), 1, 0)
        keep = jnp.full((BLK, BLK), live.astype(F32))
        if own:
            keep = jnp.where(diagonal, 0.0, keep)
            rows = own_rows
        else:
            rows = gpos[g].astype(F32)
        shift = [(g // 3 - 1).astype(F32), (lax.rem(g, 3) - 1).astype(F32)]
        axis_of = lax.broadcasted_iota(jnp.int32, (3, BLK), 0)
        rows = rows + jnp.where(axis_of == 0, shift[0], jnp.where(axis_of == 1, shift[1], 0.0))
        cols = columns(rows)
        gcols[g] = cols
        line = [rows[m:m + 1, :] for m in range(3)]
        col = [cols[:, m:m + 1] for m in range(3)]
        lane = pl.ds(pl.multiple_of(g * BLK, BLK), BLK)
        for k, b in enumerate(radial(*[line[m] - own_c[m] for m in range(3)], keep)):
            basis[k * BLK:(k + 1) * BLK, lane] = b
        for k, b in enumerate(radial(*[col[m] - own_x[m] for m in range(3)], keep)):
            basis_t[lane, k * BLK:(k + 1) * BLK] = b

    def stack_tile(g, feat):
        cols = gcols[g]
        lane = pl.ds(pl.multiple_of(g * BLK, BLK), BLK)
        h = feat.astype(F32)
        stack[lane, 0:CH] = feat
        for m in range(3):
            stack[lane, (m + 1) * CH:(m + 2) * CH] = (cols[:, m:m + 1] * h).astype(BF16)

    tile(jnp.int32(0), True)
    stack_tile(jnp.int32(OWN), feat_ref[0, 0])

    @pl.loop(1, GHOSTS)
    def _(p):
        g = lax.rem(p + OWN, GHOSTS)
        pos_copy(8 - g).wait_recv()
        tile(p, False)

    @pl.loop(1, GHOSTS)
    def _(p):
        g = lax.rem(p + OWN, GHOSTS)
        feat_copy(8 - g).wait_recv()
        stack_tile(g, gfeat[g])

    def halves(nb):
        return jnp.dot(basis[...], stack[:, nb * 2 * CH:(nb + 1) * 2 * CH], preferred_element_type=F32)

    def weigh(values, row):
        total = None
        for k in range(NRAD):
            term = rad_ref[row, k:k + 1, :] * values[k * BLK:(k + 1) * BLK]
            total = term if total is None else total + term
        return total

    first_half = halves(0)
    sum_zero = weigh(first_half[:, :CH], 0)
    sum_one = weigh(first_half[:, :CH], 1)
    moment = [weigh(first_half[:, CH:], 1)]
    second_half = halves(1)
    moment.append(weigh(second_half[:, :CH], 1))
    moment.append(weigh(second_half[:, CH:], 1))

    first_bf = sum_zero.astype(BF16)
    second = [(moment[m] - own_c[m] * sum_one).astype(BF16) for m in range(3)]
    second_all = jnp.concatenate(second, axis=0)
    quadratic = jnp.dot(second_all, square_ref[...], preferred_element_type=F32)
    quad = [quadratic[m * BLK:(m + 1) * BLK] for m in range(3)]
    second_f = [s.astype(F32) for s in second]
    linear = jnp.dot(first_bf, mix_ref[...], preferred_element_type=F32)
    square_sum = quad[0] * second_f[0] + quad[1] * second_f[1] + quad[2] * second_f[2]
    updated_ref[0, 0] = (linear + square_sum).astype(BF16)
    cot_f = cot.astype(F32)
    weighted = jnp.concatenate([(cot_f * s).astype(BF16) for s in second_f], axis=0)
    through = lax.dot_general(weighted, square_ref[...], nt, preferred_element_type=F32)
    grad_second = [cot_f * quad[m] + through[m * BLK:(m + 1) * BLK] for m in range(3)]
    grad_one = -(own_c[0] * grad_second[0] + own_c[1] * grad_second[1] + own_c[2] * grad_second[2])
    for k in range(NRAD):
        rows = slice(k * BLK, (k + 1) * BLK)
        w0 = rad_ref[0, k:k + 1, :]
        w1 = rad_ref[1, k:k + 1, :]
        gbasis[rows, 0:CH] = (w0 * grad_first + w1 * grad_one).astype(BF16)
        for m in range(3):
            gbasis[rows, (m + 1) * CH:(m + 2) * CH] = (w1 * grad_second[m]).astype(BF16)

    def pull(g):
        lane = pl.ds(pl.multiple_of(g * BLK, BLK), BLK)
        pulled = jnp.dot(basis_t[lane, :], gbasis[...], preferred_element_type=F32)
        cols = gcols[g]
        total = pulled[:, 0:CH]
        for m in range(3):
            total = total + cols[:, m:m + 1] * pulled[:, (m + 1) * CH:(m + 2) * CH]
        return total

    @pl.loop(1, GHOSTS)
    def _(p):
        g = lax.rem(p + OWN, GHOSTS)
        out_grad[g] = pull(g).astype(BF16)
        grad_copy(g).start()

    total = pull(jnp.int32(OWN))
    for g in others:
        grad_copy(8 - g).wait_recv()
        total = total + in_grad[g].astype(F32)
    grad_ref[0, 0] = total
    for g in others:
        pos_copy(g).wait_send()
        feat_copy(g).wait_send()
        grad_copy(g).wait_send()


def solution(mesh):
    nx, ny = mesh.shape["gx"], mesh.shape["gy"]

    def body(positions, features, senders, counts, radial_w, mix_w, square_w, cotangent):
        vmem = pl.BlockSpec(memory_space=pltpu.VMEM)
        smem = pl.BlockSpec(memory_space=pltpu.SMEM)
        return pl.pallas_call(
            functools.partial(kernel, nx, ny),
            out_shape=(
                jax.ShapeDtypeStruct(features.shape, BF16),
                jax.ShapeDtypeStruct(features.shape, F32),
            ),
            in_specs=[vmem, vmem, smem, smem, vmem, vmem, vmem, vmem],
            out_specs=(vmem, vmem),
            scratch_shapes=[
                pltpu.VMEM((GHOSTS, 3, BLK), BF16),
                pltpu.VMEM((GHOSTS, BLK, CH), BF16),
                pltpu.VMEM((NRAD * BLK, GHOSTS * BLK), BF16),
                pltpu.VMEM((GHOSTS * BLK, NRAD * BLK), BF16),
                pltpu.VMEM((GHOSTS * BLK, 4 * CH), BF16),
                pltpu.VMEM((NRAD * BLK, 4 * CH), BF16),
                pltpu.VMEM((GHOSTS, BLK, BLK), F32),
                pltpu.VMEM((GHOSTS, BLK, CH), BF16),
                pltpu.VMEM((GHOSTS, BLK, CH), BF16),
            ] + [pltpu.SemaphoreType.DMA((GHOSTS,))] * 6,
            compiler_params=pltpu.CompilerParams(collective_id=0, has_side_effects=True),
            name="layer",
        )(positions, features, senders, counts, radial_w, mix_w, square_w, cotangent)

    placed = (
        P("gx", "gy", None, None),
        P("gx", "gy", None, None),
        P("gx", "gy", None, None),
        P("gx", "gy", None),
        P(),
        P(),
        P(),
        P("gx", "gy", None, None),
    )
    return jax.shard_map(
        body,
        mesh=mesh,
        in_specs=placed,
        out_specs=(P("gx", "gy", None, None), P("gx", "gy", None, None)),
        check_vma=False,
    )
```

profile of v0, /device:TPU:2, one launch (start us, length us, event | category | flops | bytes accessed | tf_op | source)
XLA Modules:
  0.0 44.1 jit_solution(16456525807195936074)
XLA Ops:
  1.3 40.7 %layer.1 = (bf16[1,1,128,128]{3,2,1,0:T(8,128)(2,1)}, f32[1,1,128,128]{3,2,1,0:T(8,128)}) custom-call(bf16[1,1,3,128]{3,2,1,0:T(4,128)(2,1)} %pos_ref.1, bf16[1,1,128,128]{3,2,1,0:T(8,128)(2,1)} %feat_ref.1, s32[1,1,1,8]{3,2,1,0:T(1,128)} %senders_ref.1, s32[1,1,1]{2,1,0:T(1,128)S(6)} %copy.12.counts_ref, f32[2,8,128]{2,1,0:T(8,128)} %rad_ref.1, ...), custom_call_target="tpu_custom_call" | custom-call | tf_op jit(solution)/shard_map/layer/pallas_call | solution.py:214
  42.0 0.0 copy-start
  42.0 1.4 %copy.13 = bf16[1,1,128,128]{3,2,1,0:T(8,128)(2,1)} copy(bf16[1,1,128,128]{3,2,1,0:T(8,128)(2,1)} %get-tuple-element.4) | data formatting | bytes 65536
  43.5 0.0 copy-done
  43.5 0.6 %copy.14 = f32[1,1,128,128]{3,2,1,0:T(8,128)} copy(f32[1,1,128,128]{3,2,1,0:T(8,128)S(1)} %copy-done) | data formatting | bytes 131072
Async XLA Ops:
  42.0 1.4 %copy-start = (f32[1,1,128,128]{3,2,1,0:T(8,128)S(1)}, f32[1,1,128,128]{3,2,1,0:T(8,128)}, u32[]{:S(2)}) copy-start(f32[1,1,128,128]{3,2,1,0:T(8,128)} %get-tuple-element.5) | copy-start | bytes 196612
where the time goes:
time: 44.3 us; the launch traced here: 44.1 us
  Pallas kernels  40.7 us (92%)
  local copies, waits for them, and re-layouts  2.04 us (5%)
  between operations  1.29 us (3%)
    pallas_call x1, Pallas kernels, body(): pl.pallas_call(functools.partial(kernel, nx, ny), out_shape=(jax.ShapeDty...  40.7 us
    unnamed x4, local copies, waits for them, and re-layouts  2.04 us

commit v1 on v0

v1 whole, which is shorter than its diff:
```python
import functools
import math

import jax
import jax.numpy as jnp
from jax import lax
from jax.experimental import pallas as pl
from jax.experimental.pallas import tpu as pltpu
from jax.sharding import PartitionSpec as P

MESH = pl.DeviceIdType.MESH
BLK = 128
CH = 128
NRAD = 8
GHOSTS = 9
F32 = jnp.float32
BF16 = jnp.bfloat16
NT = (((1,), (1,)), ((), ()))

SERIES = [(-1.0) ** (n + 1) * math.pi ** (2 * n + 1) / math.factorial(2 * n + 1) for n in range(7)]

DX = [0, -1, 1]
DY = [0, 1, -1]


def mirrored(p):
    r, q = p // 3, p % 3
    return 3 * ((3 - r) % 3) + (3 - q) % 3


def radial(dx, dy, dz, keep):
    dist = jnp.sqrt(dx * dx + dy * dy + dz * dz)
    u = jnp.minimum(dist, 1.0)
    one_minus = 1.0 - u
    value = one_minus * one_minus * keep
    v = u - 0.5
    v2 = v * v
    acc = jnp.full_like(v2, SERIES[6])
    for coef in SERIES[5::-1]:
        acc = acc * v2 + coef
    cosine = acc * v
    twice = cosine + cosine
    out = [value, value * cosine]
    for _ in range(NRAD - 2):
        out.append(twice * out[-1] - out[-2])
    return [b.astype(BF16) for b in out]


def flipped(block):
    return block.astype(F32).T.astype(BF16)


def kernel(
    nx, ny,
    pos_hbm, feat_hbm, senders_hbm, counts_hbm, rad_hbm, mix_hbm, square_hbm, cot_hbm,
    updated_ref, grad_ref,
    pos, feat, senders, counts, rad, mix, square, cot,
    gpos, stack, basis, rows, gbasis, far_pos, far_feat, out_grad, in_grad,
    weight, own_col, cot_t, mix_t, square_t, grad_first, sums,
    local, psend, precv, fsend, frecv, gsend, grecv, far_precv, far_frecv, relay_psend, relay_fsend, ready,
):
    gx = lax.axis_index("gx")
    gy = lax.axis_index("gy")
    half = ny // 2
    is_down = (gy == 0) | (gy == half)
    is_up = (gy == half - 1) | (gy == ny - 1)

    def cell(dx, dy):
        return (lax.rem(gx + dx + nx, nx), lax.rem(gy + dy + ny, ny))

    def peer(p):
        return cell(DX[p % 3], DY[p // 3])

    loads = [
        pltpu.make_async_copy(src, dst, local.at[n])
        for n, (src, dst) in enumerate([
            (feat_hbm, feat), (pos_hbm, pos), (cot_hbm, cot), (rad_hbm, rad),
            (mix_hbm, mix), (square_hbm, square), (senders_hbm, senders), (counts_hbm, counts),
        ])
    ]
    for load in loads:
        load.start()

    barrier = pltpu.get_barrier_semaphore()

    def announce(device):
        pl.semaphore_signal(barrier, inc=1, device_id=device, device_id_type=MESH)

    for p in range(1, 3):
        announce(peer(p))
    for p in range(3, 6):
        @pl.when(jnp.logical_not(is_up))
        def _():
            announce(peer(p))
    for p in range(6, 9):
        announce(peer(p))

        @pl.when(is_down)
        def _():
            announce(cell(DX[p % 3], half))

    @pl.when(is_down)
    def _():
        announce(cell(0, half - 1))

    loads[0].wait()
    own_feat = flipped(feat[0, 0])
    stack[0, 0:CH, :] = own_feat
    loads[1].wait()
    pl.semaphore_wait(barrier, 8 + jnp.where(is_up, 1, 0))

    @pl.when(is_up)
    def _():
        pl.semaphore_signal(ready, inc=1, device_id=cell(0, 1 - half), device_id_type=MESH)

    def pos_copy(p):
        return pltpu.make_async_remote_copy(
            src_ref=pos.at[0, 0], dst_ref=gpos.at[mirrored(p)], send_sem=psend.at[p],
            recv_sem=precv.at[mirrored(p)], device_id=peer(p), device_id_type=MESH)

    def feat_copy(p):
        return pltpu.make_async_remote_copy(
            src_ref=stack.at[0, pl.ds(0, CH)], dst_ref=stack.at[mirrored(p), pl.ds(0, CH)], send_sem=fsend.at[p],
            recv_sem=frecv.at[mirrored(p)], device_id=peer(p), device_id_type=MESH)

    def far_copy(kind, q):
        there = (3 - q) % 3
        if kind == 0:
            return pltpu.make_async_remote_copy(
                src_ref=pos.at[0, 0], dst_ref=far_pos.at[there], send_sem=psend.at[6 + q],
                recv_sem=far_precv.at[there], device_id=cell(DX[q], half), device_id_type=MESH)
        return pltpu.make_async_remote_copy(
            src_ref=stack.at[0, pl.ds(0, CH)], dst_ref=far_feat.at[there], send_sem=fsend.at[6 + q],
            recv_sem=far_frecv.at[there], device_id=cell(DX[q], half), device_id_type=MESH)

    def relay_copy(kind, q):
        if kind == 0:
            return pltpu.make_async_remote_copy(
                src_ref=far_pos.at[q], dst_ref=gpos.at[3 + q], send_sem=relay_psend.at[q],
                recv_sem=precv.at[3 + q], device_id=cell(0, half - 1), device_id_type=MESH)
        return pltpu.make_async_remote_copy(
            src_ref=far_feat.at[q], dst_ref=stack.at[3 + q, pl.ds(0, CH)], send_sem=relay_fsend.at[q],
            recv_sem=frecv.at[3 + q], device_id=cell(0, half - 1), device_id_type=MESH)

    def pos_arrival(p):
        pltpu.make_async_remote_copy(
            src_ref=pos.at[0, 0], dst_ref=gpos.at[p], send_sem=psend.at[p],
            recv_sem=precv.at[p], device_id=peer(1), device_id_type=MESH).wait_recv()

    def feat_arrival(p):
        pltpu.make_async_remote_copy(
            src_ref=stack.at[0, pl.ds(0, CH)], dst_ref=stack.at[p, pl.ds(0, CH)], send_sem=fsend.at[p],
            recv_sem=frecv.at[p], device_id=peer(1), device_id_type=MESH).wait_recv()

    def grad_copy(p):
        return pltpu.make_async_remote_copy(
            src_ref=out_grad.at[p], dst_ref=in_grad.at[mirrored(p)], send_sem=gsend.at[p],
            recv_sem=grecv.at[mirrored(p)], device_id=peer(p), device_id_type=MESH)

    for kind in range(2):
        for p in (3, 4, 5, 6, 7, 8, 1, 2):
            direct = (pos_copy, feat_copy)[kind]
            if p < 6:
                direct(p).start()
            else:
                @pl.when(is_down)
                def _():
                    far_copy(kind, p - 6).start()

                @pl.when(jnp.logical_not(is_down))
                def _():
                    direct(p).start()

    own_rows = pos[0, 0].astype(F32)
    own_x = [own_rows[m:m + 1, :] for m in range(3)]
    columns = jnp.concatenate([own_rows, jnp.zeros((BLK - 3, BLK), F32)], axis=0).T
    for m in range(3):
        own_col[m] = jnp.broadcast_to(columns[:, m:m + 1], (BLK, BLK))
    for load in loads[2:]:
        load.wait()
    count = counts[0, 0, 0]
    radial_rows = jnp.concatenate([rad[0], rad[1], jnp.zeros((BLK - 2 * NRAD, CH), F32)], axis=0).T
    for n in range(2 * NRAD):
        weight[n] = jnp.broadcast_to(radial_rows[:, n:n + 1], (CH, BLK))
    cot_t[...] = flipped(cot[0, 0])
    mix_t[...] = flipped(mix[...])
    square_t[...] = flipped(square[...])
    grad_first[...] = jnp.dot(mix[...], cot_t[...], preferred_element_type=F32)
    diagonal = lax.broadcasted_iota(jnp.int32, (BLK, BLK), 0) == lax.broadcasted_iota(jnp.int32, (BLK, BLK), 1)

    def tile_basis(p, own):
        dx = lax.rem(2 * lax.rem(p, 3) + 1, 3) - 1
        dy = lax.rem(lax.div(p, 3) + 1, 3) - 1
        g = 3 * (dx + 1) + dy + 1
        live = jnp.int32(0)
        for t in range(8):
            live = live + jnp.where((senders[0, 0, 0, t] == g) & (t < count), 1, 0)
        keep = jnp.full((BLK, BLK), live.astype(F32))
        if own:
            keep = jnp.where(diagonal, 0.0, keep)
        axis_of = lax.broadcasted_iota(jnp.int32, (3, BLK), 0)
        shift = jnp.where(axis_of == 0, dx.astype(F32), jnp.where(axis_of == 1, dy.astype(F32), 0.0))
        place = (pos[0, 0] if own else gpos[p]).astype(F32) + shift
        for m in range(3):
            rows[p, m:m + 1, :] = place[m:m + 1, :]
        offsets = [place[m:m + 1, :] - own_col[m] for m in range(3)]
        for k, b in enumerate(radial(*offsets, keep)):
            basis[p, k * BLK:(k + 1) * BLK, :] = b

    def tile_stack(p):
        h = stack[p, 0:CH, :].astype(F32)
        for m in range(3):
            stack[p, (m + 1) * CH:(m + 2) * CH, :] = (rows[p, m:m + 1, :] * h).astype(BF16)

    def gather(first, last):
        left = jnp.concatenate([stack[p] for p in range(first, last)], axis=1)
        for pair in range(NRAD // 2):
            span = slice(2 * pair * BLK, 2 * (pair + 1) * BLK)
            right = jnp.concatenate([basis[p, span, :] for p in range(first, last)], axis=1)
            product = lax.dot_general(left, right, NT, preferred_element_type=F32)
            for n in range(5):
                block = max(n - 1, 0)
                part = product[block * CH:(block + 1) * CH]
                w = 0 if n == 0 else NRAD
                term = weight[w + 2 * pair] * part[:, :BLK] + weight[w + 2 * pair + 1] * part[:, BLK:]
                if first == 0 and pair == 0:
                    sums[n] = term
                else:
                    sums[n] += term

    tile_basis(jnp.int32(0), True)
    tile_stack(0)

    def receive(first, last):
        @pl.loop(first, last)
        def _(p):
            pos_arrival(p)
            tile_basis(p, False)

        @pl.loop(first, last)
        def _(p):
            feat_arrival(p)
            tile_stack(p)

    receive(1, 6)
    gather(0, 6)

    @pl.when(is_down)
    def _():
        for kind in range(2):
            for q in range(3):
                far_copy(kind, q).wait_recv()
        pl.semaphore_wait(ready, 1)
        for kind in range(2):
            for q in range(3):
                relay_copy(kind, q).start()

    receive(6, 9)
    gather(6, 9)

    sum_one = sums[1]
    second = [(sums[2 + m] - own_x[m] * sum_one).astype(BF16) for m in range(3)]
    quadratic = jnp.dot(square_t[...], jnp.concatenate(second, axis=1), preferred_element_type=F32)
    quad = [quadratic[:, m * BLK:(m + 1) * BLK] for m in range(3)]
    second_f = [s.astype(F32) for s in second]
    cot_f = cot_t[...].astype(F32)
    weighted = jnp.concatenate([(cot_f * s).astype(BF16) for s in second_f], axis=1)
    through = jnp.dot(square[...], weighted, preferred_element_type=F32)
    grad_second = [cot_f * quad[m] + through[:, m * BLK:(m + 1) * BLK] for m in range(3)]
    grad_one = -(own_x[0] * grad_second[0] + own_x[1] * grad_second[1] + own_x[2] * grad_second[2])
    for k in range(NRAD):
        lanes = slice(k * BLK, (k + 1) * BLK)
        w0, w1 = weight[k], weight[NRAD + k]
        gbasis[0:CH, lanes] = (w0 * grad_first[...] + w1 * grad_one).astype(BF16)
        for m in range(3):
            gbasis[(m + 1) * CH:(m + 2) * CH, lanes] = (w1 * grad_second[m]).astype(BF16)

    def pull(blocks):
        right = jnp.concatenate([basis[p] for p in blocks], axis=1)
        pulled = jnp.dot(gbasis[...], right, preferred_element_type=F32)
        out = []
        for n, p in enumerate(blocks):
            lanes = slice(n * BLK, (n + 1) * BLK)
            total = pulled[0:CH, lanes]
            for m in range(3):
                total = total + rows[p, m:m + 1, :] * pulled[(m + 1) * CH:(m + 2) * CH, lanes]
            out.append(total)
        return out

    for blocks in ((3, 4), (5, 1), (2, 6), (7, 8)):
        for p, total in zip(blocks, pull(blocks)):
            out_grad[p] = total.astype(BF16)
            grad_copy(p).start()

    linear = jnp.dot(mix_t[...], sums[0].astype(BF16), preferred_element_type=F32)
    square_sum = quad[0] * second_f[0] + quad[1] * second_f[1] + quad[2] * second_f[2]
    updated_ref[0, 0] = (linear + square_sum).T.astype(BF16)

    total = pull((0,))[0]
    for p in (1, 2, 3, 4, 5, 6, 7, 8):
        grad_copy(mirrored(p)).wait_recv()
        total = total + in_grad[p].astype(F32)
    grad_ref[0, 0] = total.T
    for p in range(1, GHOSTS):
        pos_copy(p).wait_send()
        feat_copy(p).wait_send()
        grad_copy(p).wait_send()

    @pl.when(is_down)
    def _():
        for kind in range(2):
            for q in range(3):
                relay_copy(kind, q).wait_send()


def solution(mesh):
    nx, ny = mesh.shape["gx"], mesh.shape["gy"]

    def body(positions, features, senders, counts, radial_w, mix_w, square_w, cotangent):
        vmem = pl.BlockSpec(memory_space=pltpu.VMEM)
        hbm = pl.BlockSpec(memory_space=pl.ANY)
        dma = pltpu.SemaphoreType.DMA
        return pl.pallas_call(
            functools.partial(kernel, nx, ny),
            out_shape=(
                jax.ShapeDtypeStruct(features.shape, BF16),
                jax.ShapeDtypeStruct(features.shape, F32),
            ),
            in_specs=[hbm] * 8,
            out_specs=(vmem, vmem),
            scratch_shapes=[
                pltpu.VMEM(positions.shape, BF16),
                pltpu.VMEM(features.shape, BF16),
                pltpu.SMEM(senders.shape, jnp.int32),
                pltpu.SMEM(counts.shape, jnp.int32),
                pltpu.VMEM(radial_w.shape, F32),
                pltpu.VMEM(mix_w.shape, BF16),
                pltpu.VMEM(square_w.shape, BF16),
                pltpu.VMEM(cotangent.shape, BF16),
                pltpu.VMEM((GHOSTS, 3, BLK), BF16),
                pltpu.VMEM((GHOSTS, 4 * CH, BLK), BF16),
                pltpu.VMEM((GHOSTS, NRAD * BLK, BLK), BF16),
                pltpu.VMEM((GHOSTS, 8, BLK), F32),
                pltpu.VMEM((4 * CH, NRAD * BLK), BF16),
                pltpu.VMEM((3, 3, BLK), BF16),
                pltpu.VMEM((3, CH, BLK), BF16),
                pltpu.VMEM((GHOSTS, CH, BLK), BF16),
                pltpu.VMEM((GHOSTS, CH, BLK), BF16),
                pltpu.VMEM((2 * NRAD, CH, BLK), F32),
                pltpu.VMEM((3, BLK, BLK), F32),
                pltpu.VMEM((CH, BLK), BF16),
                pltpu.VMEM((CH, CH), BF16),
                pltpu.VMEM((CH, CH), BF16),
                pltpu.VMEM((CH, BLK), F32),
                pltpu.VMEM((5, CH, BLK), F32),
                dma((8,)),
                dma((GHOSTS,)), dma((GHOSTS,)), dma((GHOSTS,)), dma((GHOSTS,)), dma((GHOSTS,)), dma((GHOSTS,)),
                dma((3,)), dma((3,)), dma((3,)), dma((3,)),
                pltpu.SemaphoreType.REGULAR,
            ],
            compiler_params=pltpu.CompilerParams(collective_id=0, has_side_effects=True),
            name="layer",
        )(positions, features, senders, counts, radial_w, mix_w, square_w, cotangent)

    placed = (
        P("gx", "gy", None, None),
        P("gx", "gy", None, None),
        P("gx", "gy", None, None),
        P("gx", "gy", None),
        P(),
        P(),
        P(),
        P("gx", "gy", None, None),
    )
    return jax.shard_map(
        body,
        mesh=mesh,
        in_specs=placed,
        out_specs=(P("gx", "gy", None, None), P("gx", "gy", None, None)),
        check_vma=False,
    )
```

time: 44.3 us -> 38.2 us (0.86)
  Pallas kernels: 40.7 us -> 34.6 us
    pallas_call x1, Pallas kernels: 40.7 us -> 34.6 us  [body(): pl.pallas_call(functools.partial(kernel, nx, ny), out_shape=(jax.ShapeDty...]
where the time goes in v1:
time: 38.2 us; the launch traced here: 37.9 us
  Pallas kernels  34.6 us (91%)
  local copies, waits for them, and re-layouts  2.04 us (5%)
  between operations  1.29 us (3%)
    pallas_call x1, Pallas kernels, body(): pl.pallas_call(functools.partial(kernel, nx, ny), out_shape=(jax.ShapeDty...  34.6 us
    unnamed x4, local copies, waits for them, and re-layouts  2.04 us

profile of v1, /device:TPU:2, one launch (start us, length us, event | category | flops | bytes accessed | tf_op | source)
XLA Modules:
  0.0 37.9 jit_solution(6758378190761576084)
XLA Ops:
  1.3 34.6 %layer.1 = (bf16[1,1,128,128]{3,2,1,0:T(8,128)(2,1)}, f32[1,1,128,128]{3,2,1,0:T(8,128)}) custom-call(bf16[1,1,3,128]{3,2,1,0:T(4,128)(2,1)} %pos_hbm.1, bf16[1,1,128,128]{3,2,1,0:T(8,128)(2,1)} %feat_hbm.1, s32[1,1,1,8]{3,2,1,0:T(1,128)} %senders_hbm.1, s32[1,1,1]{2,1,0:T(1,128)S(6)} %copy.12.counts_hbm, f32[2,8,128]{2,1,0:T(8,128)} %rad_hbm.1, ...), custom_call_target="tpu_custom_call" | custom-call | tf_op jit(solution)/shard_map/layer/pallas_call | solution.py:323
  35.9 0.0 copy-start
  35.9 1.4 %copy.13 = bf16[1,1,128,128]{3,2,1,0:T(8,128)(2,1)} copy(bf16[1,1,128,128]{3,2,1,0:T(8,128)(2,1)} %get-tuple-element.4) | data formatting | bytes 65536
  37.3 0.0 copy-done
  37.3 0.6 %copy.14 = f32[1,1,128,128]{3,2,1,0:T(8,128)} copy(f32[1,1,128,128]{3,2,1,0:T(8,128)S(1)} %copy-done) | data formatting | bytes 131072
Async XLA Ops:
  35.9 1.4 %copy-start = (f32[1,1,128,128]{3,2,1,0:T(8,128)S(1)}, f32[1,1,128,128]{3,2,1,0:T(8,128)}, u32[]{:S(2)}) copy-start(f32[1,1,128,128]{3,2,1,0:T(8,128)} %get-tuple-element.5) | copy-start | bytes 196612

commit v2 on v1

--- a/solution.py
+++ b/solution.py
@@ -20,12 +20,6 @@
 SERIES = [(-1.0) ** (n + 1) * math.pi ** (2 * n + 1) / math.factorial(2 * n + 1) for n in range(7)]
 
 DX = [0, -1, 1]
-DY = [0, 1, -1]
-
-
-def mirrored(p):
-    r, q = p // 3, p % 3
-    return 3 * ((3 - r) % 3) + (3 - q) % 3
 
 
 def radial(dx, dy, dz, keep):
@@ -57,7 +51,7 @@
     pos, feat, senders, counts, rad, mix, square, cot,
     gpos, stack, basis, rows, gbasis, far_pos, far_feat, out_grad, in_grad,
     weight, own_col, cot_t, mix_t, square_t, grad_first, sums,
-    local, psend, precv, fsend, frecv, gsend, grecv, far_precv, far_frecv, relay_psend, relay_fsend, ready,
+    local, psend, precv, fsend, frecv, gsend, grecv, far_precv, far_frecv, ready,
 ):
     gx = lax.axis_index("gx")
     gy = lax.axis_index("gy")
@@ -65,18 +59,28 @@
     is_down = (gy == 0) | (gy == half)
     is_up = (gy == half - 1) | (gy == ny - 1)
 
+    sign = jnp.where(is_up, -1, 1)
+
     def cell(dx, dy):
         return (lax.rem(gx + dx + nx, nx), lax.rem(gy + dy + ny, ny))
 
-    def peer(p):
-        return cell(DX[p % 3], DY[p // 3])
+    def step_y(r):
+        return jnp.where(r == 0, 0, jnp.where(r == 1, sign, -sign))
+
+    def peer(r, q):
+        return cell(DX[q], step_y(r))
+
+    def mirrored(r, q):
+        dy = step_y(r)
+        there = lax.rem(gy + dy + ny, ny)
+        sign_there = jnp.where((there == half - 1) | (there == ny - 1), -1, 1)
+        return 3 * jnp.where(dy == 0, 0, jnp.where(dy == -sign_there, 1, 2)) + (3 - q) % 3
 
     loads = [
         pltpu.make_async_copy(src, dst, local.at[n])
-        for n, (src, dst) in enumerate([
-            (feat_hbm, feat), (pos_hbm, pos), (cot_hbm, cot), (rad_hbm, rad),
-            (mix_hbm, mix), (square_hbm, square), (senders_hbm, senders), (counts_hbm, counts),
-        ])
+        for n, src, dst in (
+            (0, feat_hbm, feat), (1, pos_hbm, pos), (2, cot_hbm, cot), (2, mix_hbm, mix), (2, square_hbm, square),
+            (3, rad_hbm, rad), (4, senders_hbm, senders), (5, counts_hbm, counts))
     ]
     for load in loads:
         load.start()
@@ -86,18 +90,16 @@
     def announce(device):
         pl.semaphore_signal(barrier, inc=1, device_id=device, device_id_type=MESH)
 
-    for p in range(1, 3):
-        announce(peer(p))
-    for p in range(3, 6):
+    for r, q in ((0, 1), (0, 2), (1, 0), (1, 1), (1, 2)):
+        announce(peer(r, q))
+    for q in range(3):
         @pl.when(jnp.logical_not(is_up))
         def _():
-            announce(peer(p))
-    for p in range(6, 9):
-        announce(peer(p))
+            announce(peer(2, q))
 
         @pl.when(is_down)
         def _():
-            announce(cell(DX[p % 3], half))
+            announce(cell(DX[q], half))
 
     @pl.when(is_down)
     def _():
@@ -113,70 +115,71 @@
     def _():
         pl.semaphore_signal(ready, inc=1, device_id=cell(0, 1 - half), device_id_type=MESH)
 
-    def pos_copy(p):
+    def halo_copy(kind, r, q):
+        p, there = 3 * r + q, mirrored(r, q)
+        if kind == 0:
+            return pltpu.make_async_remote_copy(
+                src_ref=pos.at[0, 0], dst_ref=gpos.at[there], send_sem=psend,
+                recv_sem=precv.at[there // 6], device_id=peer(r, q), device_id_type=MESH)
         return pltpu.make_async_remote_copy(
-            src_ref=pos.at[0, 0], dst_ref=gpos.at[mirrored(p)], send_sem=psend.at[p],
-            recv_sem=precv.at[mirrored(p)], device_id=peer(p), device_id_type=MESH)
-
-    def feat_copy(p):
-        return pltpu.make_async_remote_copy(
-            src_ref=stack.at[0, pl.ds(0, CH)], dst_ref=stack.at[mirrored(p), pl.ds(0, CH)], send_sem=fsend.at[p],
-            recv_sem=frecv.at[mirrored(p)], device_id=peer(p), device_id_type=MESH)
+            src_ref=stack.at[0, pl.ds(0, CH)], dst_ref=stack.at[there, pl.ds(0, CH)], send_sem=fsend,
+            recv_sem=frecv.at[there], device_id=peer(r, q), device_id_type=MESH)
 
     def far_copy(kind, q):
         there = (3 - q) % 3
         if kind == 0:
             return pltpu.make_async_remote_copy(
-                src_ref=pos.at[0, 0], dst_ref=far_pos.at[there], send_sem=psend.at[6 + q],
-                recv_sem=far_precv.at[there], device_id=cell(DX[q], half), device_id_type=MESH)
+                src_ref=pos.at[0, 0], dst_ref=far_pos.at[there], send_sem=psend,
+                recv_sem=far_precv, device_id=cell(DX[q], half), device_id_type=MESH)
         return pltpu.make_async_remote_copy(
-            src_ref=stack.at[0, pl.ds(0, CH)], dst_ref=far_feat.at[there], send_sem=fsend.at[6 + q],
-            recv_sem=far_frecv.at[there], device_id=cell(DX[q], half), device_id_type=MESH)
+            src_ref=stack.at[0, pl.ds(0, CH)], dst_ref=far_feat.at[there], send_sem=fsend,
+            recv_sem=far_frecv, device_id=cell(DX[q], half), device_id_type=MESH)
 
     def relay_copy(kind, q):
         if kind == 0:
             return pltpu.make_async_remote_copy(
-                src_ref=far_pos.at[q], dst_ref=gpos.at[3 + q], send_sem=relay_psend.at[q],
-                recv_sem=precv.at[3 + q], device_id=cell(0, half - 1), device_id_type=MESH)
+                src_ref=far_pos.at[q], dst_ref=gpos.at[6 + q], send_sem=psend,
+                recv_sem=precv.at[1], device_id=cell(0, half - 1), device_id_type=MESH)
         return pltpu.make_async_remote_copy(
-            src_ref=far_feat.at[q], dst_ref=stack.at[3 + q, pl.ds(0, CH)], send_sem=relay_fsend.at[q],
-            recv_sem=frecv.at[3 + q], device_id=cell(0, half - 1), device_id_type=MESH)
-
-    def pos_arrival(p):
+            src_ref=far_feat.at[q], dst_ref=stack.at[6 + q, pl.ds(0, CH)], send_sem=fsend,
+            recv_sem=frecv.at[6 + q], device_id=cell(0, half - 1), device_id_type=MESH)
+
+    def sent(ref, sem):
         pltpu.make_async_remote_copy(
-            src_ref=pos.at[0, 0], dst_ref=gpos.at[p], send_sem=psend.at[p],
-            recv_sem=precv.at[p], device_id=peer(1), device_id_type=MESH).wait_recv()
-
-    def feat_arrival(p):
+            src_ref=ref, dst_ref=ref, send_sem=sem, recv_sem=far_precv,
+            device_id=peer(0, 1), device_id_type=MESH).wait_send()
+
+    def arrived(ref, sem):
         pltpu.make_async_remote_copy(
-            src_ref=stack.at[0, pl.ds(0, CH)], dst_ref=stack.at[p, pl.ds(0, CH)], send_sem=fsend.at[p],
-            recv_sem=frecv.at[p], device_id=peer(1), device_id_type=MESH).wait_recv()
-
-    def grad_copy(p):
+            src_ref=ref, dst_ref=ref, send_sem=gsend, recv_sem=sem,
+            device_id=peer(0, 1), device_id_type=MESH).wait_recv()
+
+    def grad_copy(r, q):
+        p, there = 3 * r + q, mirrored(r, q)
         return pltpu.make_async_remote_copy(
-            src_ref=out_grad.at[p], dst_ref=in_grad.at[mirrored(p)], send_sem=gsend.at[p],
-            recv_sem=grecv.at[mirrored(p)], device_id=peer(p), device_id_type=MESH)
+            src_ref=out_grad.at[p], dst_ref=in_grad.at[there], send_sem=gsend,
+            recv_sem=grecv.at[there // 6], device_id=peer(r, q), device_id_type=MESH)
 
     for kind in range(2):
-        for p in (3, 4, 5, 6, 7, 8, 1, 2):
-            direct = (pos_copy, feat_copy)[kind]
-            if p < 6:
-                direct(p).start()
-            else:
-                @pl.when(is_down)
-                def _():
-                    far_copy(kind, p - 6).start()
-
-                @pl.when(jnp.logical_not(is_down))
-                def _():
-                    direct(p).start()
+        for q in range(3):
+            @pl.when(is_down)
+            def _():
+                far_copy(kind, q).start()
+
+            @pl.when(jnp.logical_not(is_down))
+            def _():
+                halo_copy(kind, 2, q).start()
+
+        for r, q in ((1, 0), (1, 1), (1, 2), (0, 1), (0, 2)):
+            halo_copy(kind, r, q).start()
 
     own_rows = pos[0, 0].astype(F32)
     own_x = [own_rows[m:m + 1, :] for m in range(3)]
     columns = jnp.concatenate([own_rows, jnp.zeros((BLK - 3, BLK), F32)], axis=0).T
     for m in range(3):
         own_col[m] = jnp.broadcast_to(columns[:, m:m + 1], (BLK, BLK))
-    for load in loads[2:]:
+    pltpu.make_async_copy(far_feat, far_feat, local.at[2]).wait()
+    for load in loads[5:]:
         load.wait()
     count = counts[0, 0, 0]
     radial_rows = jnp.concatenate([rad[0], rad[1], jnp.zeros((BLK - 2 * NRAD, CH), F32)], axis=0).T
@@ -190,7 +193,7 @@
 
     def tile_basis(p, own):
         dx = lax.rem(2 * lax.rem(p, 3) + 1, 3) - 1
-        dy = lax.rem(lax.div(p, 3) + 1, 3) - 1
+        dy = step_y(lax.div(p, 3))
         g = 3 * (dx + 1) + dy + 1
         live = jnp.int32(0)
         for t in range(8):
@@ -232,29 +235,29 @@
     tile_stack(0)
 
     def receive(first, last):
+        arrived(gpos.at[pl.ds(first, last - first)], precv.at[first // 6])
+
         @pl.loop(first, last)
         def _(p):
-            pos_arrival(p)
             tile_basis(p, False)
 
         @pl.loop(first, last)
         def _(p):
-            feat_arrival(p)
+            arrived(stack.at[p, pl.ds(0, CH)], frecv.at[p])
             tile_stack(p)
 
     receive(1, 6)
-    gather(0, 6)
 
     @pl.when(is_down)
     def _():
-        for kind in range(2):
-            for q in range(3):
-                far_copy(kind, q).wait_recv()
+        arrived(far_pos, far_precv)
+        arrived(far_feat, far_frecv)
         pl.semaphore_wait(ready, 1)
         for kind in range(2):
             for q in range(3):
                 relay_copy(kind, q).start()
 
+    gather(0, 6)
     receive(6, 9)
     gather(6, 9)
 
@@ -287,45 +290,44 @@
             out.append(total)
         return out
 
-    for blocks in ((3, 4), (5, 1), (2, 6), (7, 8)):
-        for p, total in zip(blocks, pull(blocks)):
-            out_grad[p] = total.astype(BF16)
-            grad_copy(p).start()
+    first = jnp.where(is_up, 2, 1)
+    for n, r in enumerate((first, 3 - first)):
+        blocks = [(r, 0), (r, 1), (r, 2), (0, n + 1)]
+        totals = pull([3 * row + q for row, q in blocks])
+        for (row, q), total in zip(blocks, totals):
+            out_grad[3 * row + q] = total.astype(BF16)
+        for row, q in blocks:
+            grad_copy(row, q).start()
 
     linear = jnp.dot(mix_t[...], sums[0].astype(BF16), preferred_element_type=F32)
     square_sum = quad[0] * second_f[0] + quad[1] * second_f[1] + quad[2] * second_f[2]
     updated_ref[0, 0] = (linear + square_sum).T.astype(BF16)
-
     total = pull((0,))[0]
-    for p in (1, 2, 3, 4, 5, 6, 7, 8):
-        grad_copy(mirrored(p)).wait_recv()
-        total = total + in_grad[p].astype(F32)
+    for first, last in ((1, 6), (6, 9)):
+        arrived(in_grad.at[pl.ds(first, last - first)], grecv.at[first // 6])
+        for p in range(first, last):
+            total = total + in_grad[p].astype(F32)
     grad_ref[0, 0] = total.T
-    for p in range(1, GHOSTS):
-        pos_copy(p).wait_send()
-        feat_copy(p).wait_send()
-        grad_copy(p).wait_send()
+    sent(gpos.at[pl.ds(1, 8)], psend)
+    sent(in_grad.at[pl.ds(1, 8)], fsend)
+    sent(in_grad.at[pl.ds(1, 8)], gsend)
 
     @pl.when(is_down)
     def _():
-        for kind in range(2):
-            for q in range(3):
-                relay_copy(kind, q).wait_send()
+        sent(far_pos, psend)
+        sent(far_feat, fsend)
 
 
 def solution(mesh):
     nx, ny = mesh.shape["gx"], mesh.shape["gy"]
 
     def body(positions, features, senders, counts, radial_w, mix_w, square_w, cotangent):
+        hbm = pl.BlockSpec(memory_space=pltpu.HBM)
+        dma = pltpu.SemaphoreType.DMA
         vmem = pl.BlockSpec(memory_space=pltpu.VMEM)
-        hbm = pl.BlockSpec(memory_space=pl.ANY)
-        dma = pltpu.SemaphoreType.DMA
         return pl.pallas_call(
             functools.partial(kernel, nx, ny),
-            out_shape=(
-                jax.ShapeDtypeStruct(features.shape, BF16),
-                jax.ShapeDtypeStruct(features.shape, F32),
-            ),
+            out_shape=(pltpu.VMEM(features.shape, BF16), pltpu.VMEM(features.shape, F32)),
             in_specs=[hbm] * 8,
             out_specs=(vmem, vmem),
             scratch_shapes=[
@@ -353,9 +355,9 @@
                 pltpu.VMEM((CH, CH), BF16),
                 pltpu.VMEM((CH, BLK), F32),
                 pltpu.VMEM((5, CH, BLK), F32),
-                dma((8,)),
-                dma((GHOSTS,)), dma((GHOSTS,)), dma((GHOSTS,)), dma((GHOSTS,)), dma((GHOSTS,)), dma((GHOSTS,)),
-                dma((3,)), dma((3,)), dma((3,)), dma((3,)),
+                dma((6,)),
+                dma, dma((2,)), dma, dma((GHOSTS,)), dma, dma((2,)),
+                dma, dma,
                 pltpu.SemaphoreType.REGULAR,
             ],
             compiler_params=pltpu.CompilerParams(collective_id=0, has_side_effects=True),

time: 38.2 us -> 35.3 us (0.924)
  Pallas kernels: 34.6 us -> 32.6 us
  local copies, waits for them, and re-layouts: 2.04 us -> 1.25 us
    pallas_call x1, Pallas kernels: 34.6 us -> 32.6 us  [body(): pl.pallas_call(functools.partial(kernel, nx, ny), out_shape=(pltpu.VMEM(f...]
    unnamed x4 -> x2, local copies, waits for them, and re-layouts: 2.04 us -> 1.25 us
where the time goes in v2:
time: 35.3 us; the launch traced here: 35.1 us
  Pallas kernels  32.6 us (92%)
  between operations  1.29 us (4%)
  local copies, waits for them, and re-layouts  1.25 us (4%)
    pallas_call x1, Pallas kernels, body(): pl.pallas_call(functools.partial(kernel, nx, ny), out_shape=(pltpu.VMEM(f...  32.6 us
    unnamed x2, local copies, waits for them, and re-layouts  1.25 us

profile of v2, /device:TPU:2, one launch (start us, length us, event | category | flops | bytes accessed | tf_op | source)
XLA Modules:
  0.0 35.1 jit_solution(3134799354712528327)
XLA Ops:
  1.3 32.6 %layer.1 = (bf16[1,1,128,128]{3,2,1,0:T(8,128)(2,1)S(1)}, f32[1,1,128,128]{3,2,1,0:T(8,128)S(1)}) custom-call(bf16[1,1,3,128]{3,2,1,0:T(4,128)(2,1)} %pos_hbm.1, bf16[1,1,128,128]{3,2,1,0:T(8,128)(2,1)} %feat_hbm.1, s32[1,1,1,8]{3,2,1,0:T(1,128)} %senders_hbm.1, s32[1,1,1]{2,1,0:T(1,128)S(6)} %copy.14.counts_hbm, f32[2,8,128]{2,1,0:T(8,128)} %rad_hbm.1, ...), custom_call_target="tpu_custom_call" | custom-call | tf_op jit(solution)/shard_map/layer/pallas_call | solution.py:328
  33.9 0.6 %copy.12 = bf16[1,1,128,128]{3,2,1,0:T(8,128)(2,1)} copy(bf16[1,1,128,128]{3,2,1,0:T(8,128)(2,1)S(1)} %get-tuple-element.2) | data formatting | bytes 65536
  34.5 0.6 %copy.13 = f32[1,1,128,128]{3,2,1,0:T(8,128)} copy(f32[1,1,128,128]{3,2,1,0:T(8,128)S(1)} %get-tuple-element.3) | data formatting | bytes 131072

commit v3 on v2

--- a/solution.py
+++ b/solution.py
@@ -161,17 +161,25 @@
             recv_sem=grecv.at[there // 6], device_id=peer(r, q), device_id_type=MESH)
 
     for kind in range(2):
-        for q in range(3):
-            @pl.when(is_down)
-            def _():
+        @pl.when(is_up)
+        def _():
+            for r, q in ((2, 0), (0, 1), (0, 2), (2, 1), (2, 2), (1, 1), (1, 2), (1, 0)):
+                halo_copy(kind, r, q).start()
+
+        @pl.when(is_down)
+        def _():
+            for q in (1, 2, 0):
                 far_copy(kind, q).start()
 
-            @pl.when(jnp.logical_not(is_down))
-            def _():
+        @pl.when(jnp.logical_not(is_up))
+        def _():
+            for r, q in ((1, 1), (1, 2), (1, 0), (0, 1), (0, 2)):
+                halo_copy(kind, r, q).start()
+
+        @pl.when(jnp.logical_not(is_up | is_down))
+        def _():
+            for q in (1, 2, 0):
                 halo_copy(kind, 2, q).start()
-
-        for r, q in ((1, 0), (1, 1), (1, 2), (0, 1), (0, 2)):
-            halo_copy(kind, r, q).start()
 
     own_rows = pos[0, 0].astype(F32)
     own_x = [own_rows[m:m + 1, :] for m in range(3)]
@@ -292,7 +300,7 @@
 
     first = jnp.where(is_up, 2, 1)
     for n, r in enumerate((first, 3 - first)):
-        blocks = [(r, 0), (r, 1), (r, 2), (0, n + 1)]
+        blocks = [(r, 1), (r, 2), (r, 0), (0, n + 1)]
         totals = pull([3 * row + q for row, q in blocks])
         for (row, q), total in zip(blocks, totals):
             out_grad[3 * row + q] = total.astype(BF16)

time: 35.3 us -> 35.1 us (level)
  the two profiles are of different devices: /device:TPU:2 before, /device:TPU:8 now
where the time goes in v3:
time: 35.1 us; the launch traced here: 34.9 us
  Pallas kernels  32.3 us (92%)
  between operations  1.29 us (4%)
  local copies, waits for them, and re-layouts  1.25 us (4%)
    pallas_call x1, Pallas kernels, body(): pl.pallas_call(functools.partial(kernel, nx, ny), out_shape=(pltpu.VMEM(f...  32.3 us
    unnamed x2, local copies, waits for them, and re-layouts  1.25 us

profile of v3, /device:TPU:8, one launch (start us, length us, event | category | flops | bytes accessed | tf_op | source)
XLA Modules:
  0.0 34.9 jit_solution(792171923813905324)
XLA Ops:
  1.3 32.3 %layer.1 = (bf16[1,1,128,128]{3,2,1,0:T(8,128)(2,1)S(1)}, f32[1,1,128,128]{3,2,1,0:T(8,128)S(1)}) custom-call(bf16[1,1,3,128]{3,2,1,0:T(4,128)(2,1)} %pos_hbm.1, bf16[1,1,128,128]{3,2,1,0:T(8,128)(2,1)} %feat_hbm.1, s32[1,1,1,8]{3,2,1,0:T(1,128)} %senders_hbm.1, s32[1,1,1]{2,1,0:T(1,128)S(6)} %copy.14.counts_hbm, f32[2,8,128]{2,1,0:T(8,128)} %rad_hbm.1, ...), custom_call_target="tpu_custom_call" | custom-call | tf_op jit(solution)/shard_map/layer/pallas_call | solution.py:336
  33.6 0.6 %copy.12 = bf16[1,1,128,128]{3,2,1,0:T(8,128)(2,1)} copy(bf16[1,1,128,128]{3,2,1,0:T(8,128)(2,1)S(1)} %get-tuple-element.2) | data formatting | bytes 65536
  34.2 0.6 %copy.13 = f32[1,1,128,128]{3,2,1,0:T(8,128)} copy(f32[1,1,128,128]{3,2,1,0:T(8,128)S(1)} %get-tuple-element.3) | data formatting | bytes 131072

commit v4 on v3

--- a/solution.py
+++ b/solution.py
@@ -58,6 +58,9 @@
     half = ny // 2
     is_down = (gy == 0) | (gy == half)
     is_up = (gy == half - 1) | (gy == ny - 1)
+    is_next = (gy == half - 2) | (gy == ny - 2)
+    at_end = is_up & (lax.rem(gx, 4) == 3)
+    near = jnp.where(lax.rem(gx, 4) == 0, 2, 1)
 
     sign = jnp.where(is_up, -1, 1)
 
@@ -82,9 +85,6 @@
             (0, feat_hbm, feat), (1, pos_hbm, pos), (2, cot_hbm, cot), (2, mix_hbm, mix), (2, square_hbm, square),
             (3, rad_hbm, rad), (4, senders_hbm, senders), (5, counts_hbm, counts))
     ]
-    for load in loads:
-        load.start()
-
     barrier = pltpu.get_barrier_semaphore()
 
     def announce(device):
@@ -105,6 +105,8 @@
     def _():
         announce(cell(0, half - 1))
 
+    for load in loads:
+        load.start()
     loads[0].wait()
     own_feat = flipped(feat[0, 0])
     stack[0, 0:CH, :] = own_feat
@@ -120,7 +122,7 @@
         if kind == 0:
             return pltpu.make_async_remote_copy(
                 src_ref=pos.at[0, 0], dst_ref=gpos.at[there], send_sem=psend,
-                recv_sem=precv.at[there // 6], device_id=peer(r, q), device_id_type=MESH)
+                recv_sem=precv.at[there], device_id=peer(r, q), device_id_type=MESH)
         return pltpu.make_async_remote_copy(
             src_ref=stack.at[0, pl.ds(0, CH)], dst_ref=stack.at[there, pl.ds(0, CH)], send_sem=fsend,
             recv_sem=frecv.at[there], device_id=peer(r, q), device_id_type=MESH)
@@ -139,7 +141,7 @@
         if kind == 0:
             return pltpu.make_async_remote_copy(
                 src_ref=far_pos.at[q], dst_ref=gpos.at[6 + q], send_sem=psend,
-                recv_sem=precv.at[1], device_id=cell(0, half - 1), device_id_type=MESH)
+                recv_sem=precv.at[6 + q], device_id=cell(0, half - 1), device_id_type=MESH)
         return pltpu.make_async_remote_copy(
             src_ref=far_feat.at[q], dst_ref=stack.at[6 + q, pl.ds(0, CH)], send_sem=fsend,
             recv_sem=frecv.at[6 + q], device_id=cell(0, half - 1), device_id_type=MESH)
@@ -160,11 +162,14 @@
             src_ref=out_grad.at[p], dst_ref=in_grad.at[there], send_sem=gsend,
             recv_sem=grecv.at[there // 6], device_id=peer(r, q), device_id_type=MESH)
 
+    def start(kind, directions):
+        for r, q in directions:
+            halo_copy(kind, r, q).start()
+
     for kind in range(2):
         @pl.when(is_up)
         def _():
-            for r, q in ((2, 0), (0, 1), (0, 2), (2, 1), (2, 2), (1, 1), (1, 2), (1, 0)):
-                halo_copy(kind, r, q).start()
+            start(kind, ((2, 1), (2, 2), (2, 0), (0, 1), (0, 2), (1, 0)))
 
         @pl.when(is_down)
         def _():
@@ -173,13 +178,15 @@
 
         @pl.when(jnp.logical_not(is_up))
         def _():
-            for r, q in ((1, 1), (1, 2), (1, 0), (0, 1), (0, 2)):
-                halo_copy(kind, r, q).start()
-
-        @pl.when(jnp.logical_not(is_up | is_down))
-        def _():
-            for q in (1, 2, 0):
-                halo_copy(kind, 2, q).start()
+            start(kind, ((1, 1), (1, 2), (1, 0)))
+
+        @pl.when(jnp.logical_not(is_up | is_next))
+        def _():
+            start(kind, ((0, 1), (0, 2)))
+
+        @pl.when(jnp.logical_not(is_up | is_next | is_down))
+        def _():
+            start(kind, ((2, 1), (2, 2), (2, 0)))
 
     own_rows = pos[0, 0].astype(F32)
     own_x = [own_rows[m:m + 1, :] for m in range(3)]
@@ -223,18 +230,18 @@
         for m in range(3):
             stack[p, (m + 1) * CH:(m + 2) * CH, :] = (rows[p, m:m + 1, :] * h).astype(BF16)
 
-    def gather(first, last):
-        left = jnp.concatenate([stack[p] for p in range(first, last)], axis=1)
+    def gather(blocks, begin=False):
+        left = jnp.concatenate([stack[p] for p in blocks], axis=1)
         for pair in range(NRAD // 2):
             span = slice(2 * pair * BLK, 2 * (pair + 1) * BLK)
-            right = jnp.concatenate([basis[p, span, :] for p in range(first, last)], axis=1)
+            right = jnp.concatenate([basis[p, span, :] for p in blocks], axis=1)
             product = lax.dot_general(left, right, NT, preferred_element_type=F32)
             for n in range(5):
                 block = max(n - 1, 0)
                 part = product[block * CH:(block + 1) * CH]
                 w = 0 if n == 0 else NRAD
                 term = weight[w + 2 * pair] * part[:, :BLK] + weight[w + 2 * pair + 1] * part[:, BLK:]
-                if first == 0 and pair == 0:
+                if begin and pair == 0:
                     sums[n] = term
                 else:
                     sums[n] += term
@@ -242,19 +249,35 @@
     tile_basis(jnp.int32(0), True)
     tile_stack(0)
 
-    def receive(first, last):
-        arrived(gpos.at[pl.ds(first, last - first)], precv.at[first // 6])
-
-        @pl.loop(first, last)
-        def _(p):
+    def receive(count, number):
+        @pl.loop(0, count)
+        def _(n):
+            p = number(n)
+            arrived(gpos.at[p], precv.at[p])
             tile_basis(p, False)
 
-        @pl.loop(first, last)
-        def _(p):
+        @pl.loop(0, count)
+        def _(n):
+            p = number(n)
             arrived(stack.at[p, pl.ds(0, CH)], frecv.at[p])
             tile_stack(p)
 
-    receive(1, 6)
+    receive(1, lambda n: n + 3)
+    gather((0, 3), begin=True)
+
+    for kind in range(2):
+        @pl.when(is_up)
+        def _():
+            start(kind, ((1, 1), (1, 2)))
+
+        @pl.when(is_next)
+        def _():
+            start(kind, ((0, 1), (0, 2), (2, 1), (2, 2), (2, 0)))
+
+    later = 3 - near
+    receive(2, lambda n: near + 3 * n)
+    gather((near, near + 3))
+    receive(2, lambda n: jnp.where(at_end, 6 + n, later + 3 * n))
 
     @pl.when(is_down)
     def _():
@@ -265,9 +288,9 @@
             for q in range(3):
                 relay_copy(kind, q).start()
 
-    gather(0, 6)
-    receive(6, 9)
-    gather(6, 9)
+    gather((jnp.where(at_end, 6, later), jnp.where(at_end, 7, later + 3)))
+    receive(3, lambda n: jnp.where(at_end, jnp.where(n == 0, 8, later + 3 * (n - 1)), 6 + n))
+    gather([jnp.where(at_end, end, other) for end, other in ((8, 6), (later, 7), (later + 3, 8))])
 
     sum_one = sums[1]
     second = [(sums[2 + m] - own_x[m] * sum_one).astype(BF16) for m in range(3)]
@@ -288,19 +311,24 @@
 
     def pull(blocks):
         right = jnp.concatenate([basis[p] for p in blocks], axis=1)
-        pulled = jnp.dot(gbasis[...], right, preferred_element_type=F32)
+        halves = [
+            jnp.dot(gbasis[2 * n * CH:2 * (n + 1) * CH, :], right, preferred_element_type=F32)
+            for n in range(2)
+        ]
         out = []
         for n, p in enumerate(blocks):
             lanes = slice(n * BLK, (n + 1) * BLK)
-            total = pulled[0:CH, lanes]
+            part = [halves[m // 2][m % 2 * CH:(m % 2 + 1) * CH, lanes] for m in range(4)]
+            total = part[0]
             for m in range(3):
-                total = total + rows[p, m:m + 1, :] * pulled[(m + 1) * CH:(m + 2) * CH, lanes]
+                total = total + rows[p, m:m + 1, :] * part[m + 1]
             out.append(total)
         return out
 
     first = jnp.where(is_up, 2, 1)
-    for n, r in enumerate((first, 3 - first)):
-        blocks = [(r, 1), (r, 2), (r, 0), (0, n + 1)]
+    second_row = 3 - first
+    for blocks in (
+        ((first, 1), (first, 2)), ((first, 0), (0, 1)), ((second_row, 1), (second_row, 2)), ((second_row, 0), (0, 2))):
         totals = pull([3 * row + q for row, q in blocks])
         for (row, q), total in zip(blocks, totals):
             out_grad[3 * row + q] = total.astype(BF16)
@@ -309,13 +337,16 @@
 
     linear = jnp.dot(mix_t[...], sums[0].astype(BF16), preferred_element_type=F32)
     square_sum = quad[0] * second_f[0] + quad[1] * second_f[1] + quad[2] * second_f[2]
-    updated_ref[0, 0] = (linear + square_sum).T.astype(BF16)
-    total = pull((0,))[0]
+    updated_ref[0] = linear.T
+    updated_ref[1] = square_sum.T
+    grad_ref[0] = pull((0,))[0].T
+    total = None
     for first, last in ((1, 6), (6, 9)):
         arrived(in_grad.at[pl.ds(first, last - first)], grecv.at[first // 6])
         for p in range(first, last):
-            total = total + in_grad[p].astype(F32)
-    grad_ref[0, 0] = total.T
+            came = in_grad[p].astype(F32)
+            total = came if total is None else total + came
+    grad_ref[1] = total.T
     sent(gpos.at[pl.ds(1, 8)], psend)
     sent(in_grad.at[pl.ds(1, 8)], fsend)
     sent(in_grad.at[pl.ds(1, 8)], gsend)
@@ -333,9 +364,9 @@
         hbm = pl.BlockSpec(memory_space=pltpu.HBM)
         dma = pltpu.SemaphoreType.DMA
         vmem = pl.BlockSpec(memory_space=pltpu.VMEM)
-        return pl.pallas_call(
+        parts = pl.pallas_call(
             functools.partial(kernel, nx, ny),
-            out_shape=(pltpu.VMEM(features.shape, BF16), pltpu.VMEM(features.shape, F32)),
+            out_shape=(pltpu.VMEM((2, BLK, CH), F32), pltpu.VMEM((2, BLK, CH), F32)),
             in_specs=[hbm] * 8,
             out_specs=(vmem, vmem),
             scratch_shapes=[
@@ -364,13 +395,16 @@
                 pltpu.VMEM((CH, BLK), F32),
                 pltpu.VMEM((5, CH, BLK), F32),
                 dma((6,)),
-                dma, dma((2,)), dma, dma((GHOSTS,)), dma, dma((2,)),
+                dma, dma((GHOSTS,)), dma, dma((GHOSTS,)), dma, dma((2,)),
                 dma, dma,
                 pltpu.SemaphoreType.REGULAR,
             ],
             compiler_params=pltpu.CompilerParams(collective_id=0, has_side_effects=True),
             name="layer",
         )(positions, features, senders, counts, radial_w, mix_w, square_w, cotangent)
+        updated, grad = lax.reduce(
+            parts, (jnp.float32(0), jnp.float32(0)), lambda a, b: (a[0] + b[0], a[1] + b[1]), (0,))
+        return updated.astype(BF16)[None, None], grad[None, None]
 
     placed = (
         P("gx", "gy", None, None),

time: 35.1 us -> 34.1 us (0.972)
  the two profiles are of different devices: /device:TPU:8 before, /device:TPU:1 now
where the time goes in v4:
time: 34.1 us; the launch traced here: 33.9 us
  Pallas kernels  31.9 us (94%)
  between operations  1.29 us (4%)
  other arithmetic  0.7 us (2%)
    pallas_call x1, Pallas kernels, body(): pl.pallas_call(functools.partial(kernel, nx, ny), out_shape=(pltpu.VMEM((...  31.9 us
    another operation x1, other arithmetic, body(): lax.reduce(parts, (jnp.float32(0), jnp.float32(0)), lambda a, b: (a[0] +...  0.7 us

profile of v4, /device:TPU:1, one launch (start us, length us, event | category | flops | bytes accessed | tf_op | source)
XLA Modules:
  0.0 33.9 jit_solution(15368883970750886634)
XLA Ops:
  1.3 31.9 %layer.1 = (f32[2,128,128]{2,1,0:T(8,128)S(1)}, f32[2,128,128]{2,1,0:T(8,128)S(1)}) custom-call(bf16[1,1,3,128]{3,2,1,0:T(4,128)(2,1)} %pos_hbm.1, bf16[1,1,128,128]{3,2,1,0:T(8,128)(2,1)} %feat_hbm.1, s32[1,1,1,8]{3,2,1,0:T(1,128)} %senders_hbm.1, s32[1,1,1]{2,1,0:T(1,128)S(6)} %copy.10.counts_hbm, f32[2,8,128]{2,1,0:T(8,128)} %rad_hbm.1, ...), custom_call_target="tpu_custom_call" | custom-call | tf_op jit(solution)/shard_map/layer/pallas_call | solution.py:367
  33.2 0.7 %reduce.15 = (bf16[128,128]{1,0:T(8,128)(2,1)}, f32[128,128]{1,0:T(8,128)}) reduce(f32[2,128,128]{2,1,0:T(8,128)S(1)} %get-tuple-element.6, f32[2,128,128]{2,1,0:T(8,128)S(1)} %get-tuple-element.7, f32[]{:T(128)} %constant.0.clone.1, f32[]{:T(128)} %constant.0.clone.1), dimensions={0}, to_apply=%region_0.0 | reduce | flops 32768 | bytes 360456 | tf_op jit(solution)/shard_map/reduce | solution.py:405

commit v5 on v4

--- a/solution.py
+++ b/solution.py
@@ -288,9 +288,15 @@
             for q in range(3):
                 relay_copy(kind, q).start()
 
-    gather((jnp.where(at_end, 6, later), jnp.where(at_end, 7, later + 3)))
-    receive(3, lambda n: jnp.where(at_end, jnp.where(n == 0, 8, later + 3 * (n - 1)), 6 + n))
-    gather([jnp.where(at_end, end, other) for end, other in ((8, 6), (later, 7), (later + 3, 8))])
+    early = jnp.where(is_down & (gx == nx - 1), 8, jnp.where(is_down & (gx == 0), 7, 6))
+    receive(1, lambda n: jnp.where(at_end, 8, early) + n)
+    gather((jnp.where(at_end, 6, later), jnp.where(at_end, 7, later + 3), jnp.where(at_end, 8, early)))
+    last = (
+        jnp.where(at_end, later, jnp.where(early == 6, 7, 6)),
+        jnp.where(at_end, later + 3, jnp.where(early == 8, 7, 8)),
+    )
+    receive(2, lambda n: jnp.where(n == 0, last[0], last[1]))
+    gather(last)
 
     sum_one = sums[1]
     second = [(sums[2 + m] - own_x[m] * sum_one).astype(BF16) for m in range(3)]

time: 34.1 us -> 33.8 us (level)
  the two profiles are of different devices: /device:TPU:1 before, /device:TPU:2 now
where the time goes in v5:
time: 33.8 us; the launch traced here: 33.6 us
  Pallas kernels  31.6 us (93%)
  between operations  1.29 us (4%)
  other arithmetic  0.7 us (2%)
    pallas_call x1, Pallas kernels, body(): pl.pallas_call(functools.partial(kernel, nx, ny), out_shape=(pltpu.VMEM((...  31.6 us
    another operation x1, other arithmetic, body(): lax.reduce(parts, (jnp.float32(0), jnp.float32(0)), lambda a, b: (a[0] +...  0.7 us

profile of v5, /device:TPU:2, one launch (start us, length us, event | category | flops | bytes accessed | tf_op | source)
XLA Modules:
  0.0 33.6 jit_solution(10346001577796654536)
XLA Ops:
  1.3 31.6 %layer.1 = (f32[2,128,128]{2,1,0:T(8,128)S(1)}, f32[2,128,128]{2,1,0:T(8,128)S(1)}) custom-call(bf16[1,1,3,128]{3,2,1,0:T(4,128)(2,1)} %pos_hbm.1, bf16[1,1,128,128]{3,2,1,0:T(8,128)(2,1)} %feat_hbm.1, s32[1,1,1,8]{3,2,1,0:T(1,128)} %senders_hbm.1, s32[1,1,1]{2,1,0:T(1,128)S(6)} %copy.10.counts_hbm, f32[2,8,128]{2,1,0:T(8,128)} %rad_hbm.1, ...), custom_call_target="tpu_custom_call" | custom-call | tf_op jit(solution)/shard_map/layer/pallas_call | solution.py:373
  32.9 0.7 %reduce.15 = (bf16[128,128]{1,0:T(8,128)(2,1)}, f32[128,128]{1,0:T(8,128)}) reduce(f32[2,128,128]{2,1,0:T(8,128)S(1)} %get-tuple-element.6, f32[2,128,128]{2,1,0:T(8,128)S(1)} %get-tuple-element.7, f32[]{:T(128)} %constant.0.clone.1, f32[]{:T(128)} %constant.0.clone.1), dimensions={0}, to_apply=%region_0.0 | reduce | flops 32768 | bytes 360456 | tf_op jit(solution)/shard_map/reduce | solution.py:411

commit v6 on v5

--- a/solution.py
+++ b/solution.py
@@ -249,18 +249,23 @@
     tile_basis(jnp.int32(0), True)
     tile_stack(0)
 
-    def receive(count, number):
-        @pl.loop(0, count)
+    def place(first, stop, number):
+        @pl.loop(first, stop)
         def _(n):
             p = number(n)
             arrived(gpos.at[p], precv.at[p])
             tile_basis(p, False)
 
-        @pl.loop(0, count)
+    def collect(first, stop, number):
+        @pl.loop(first, stop)
         def _(n):
             p = number(n)
             arrived(stack.at[p, pl.ds(0, CH)], frecv.at[p])
             tile_stack(p)
+
+    def receive(count, number):
+        place(0, count, number)
+        collect(0, count, number)
 
     receive(1, lambda n: n + 3)
     gather((0, 3), begin=True)
@@ -289,13 +294,21 @@
                 relay_copy(kind, q).start()
 
     early = jnp.where(is_down & (gx == nx - 1), 8, jnp.where(is_down & (gx == 0), 7, 6))
-    receive(1, lambda n: jnp.where(at_end, 8, early) + n)
-    gather((jnp.where(at_end, 6, later), jnp.where(at_end, 7, later + 3), jnp.where(at_end, 8, early)))
+    middle = jnp.where(at_end, 8, early)
     last = (
         jnp.where(at_end, later, jnp.where(early == 6, 7, 6)),
         jnp.where(at_end, later + 3, jnp.where(early == 8, 7, 8)),
     )
-    receive(2, lambda n: jnp.where(n == 0, last[0], last[1]))
+
+    def order(n):
+        return jnp.where(n == 0, middle, jnp.where(n == 1, last[0], last[1]))
+
+    ahead = jnp.where(at_end, 1, 3)
+    place(0, ahead, order)
+    collect(0, 1, order)
+    gather((jnp.where(at_end, 6, later), jnp.where(at_end, 7, later + 3), middle))
+    place(ahead, 3, order)
+    collect(1, 3, order)
     gather(last)
 
     sum_one = sums[1]

time: 33.8 us -> 33.6 us (level)
  the two profiles are of different devices: /device:TPU:2 before, /device:TPU:1 now
where the time goes in v6:
time: 33.6 us; the launch traced here: 33.4 us
  Pallas kernels  31.4 us (93%)
  between operations  1.29 us (4%)
  other arithmetic  0.7 us (2%)
    pallas_call x1, Pallas kernels, body(): pl.pallas_call(functools.partial(kernel, nx, ny), out_shape=(pltpu.VMEM((...  31.4 us
    another operation x1, other arithmetic, body(): lax.reduce(parts, (jnp.float32(0), jnp.float32(0)), lambda a, b: (a[0] +...  0.7 us

profile of v6, /device:TPU:1, one launch (start us, length us, event | category | flops | bytes accessed | tf_op | source)
XLA Modules:
  0.0 33.4 jit_solution(15300438812060247560)
XLA Ops:
  1.3 31.4 %layer.1 = (f32[2,128,128]{2,1,0:T(8,128)S(1)}, f32[2,128,128]{2,1,0:T(8,128)S(1)}) custom-call(bf16[1,1,3,128]{3,2,1,0:T(4,128)(2,1)} %pos_hbm.1, bf16[1,1,128,128]{3,2,1,0:T(8,128)(2,1)} %feat_hbm.1, s32[1,1,1,8]{3,2,1,0:T(1,128)} %senders_hbm.1, s32[1,1,1]{2,1,0:T(1,128)S(6)} %copy.10.counts_hbm, f32[2,8,128]{2,1,0:T(8,128)} %rad_hbm.1, ...), custom_call_target="tpu_custom_call" | custom-call | tf_op jit(solution)/shard_map/layer/pallas_call | solution.py:386
  32.7 0.7 %reduce.15 = (bf16[128,128]{1,0:T(8,128)(2,1)}, f32[128,128]{1,0:T(8,128)}) reduce(f32[2,128,128]{2,1,0:T(8,128)S(1)} %get-tuple-element.6, f32[2,128,128]{2,1,0:T(8,128)S(1)} %get-tuple-element.7, f32[]{:T(128)} %constant.0.clone.1, f32[]{:T(128)} %constant.0.clone.1), dimensions={0}, to_apply=%region_0.0 | reduce | flops 32768 | bytes 360456 | tf_op jit(solution)/shard_map/reduce | solution.py:424

commit v7 on v6

--- a/solution.py
+++ b/solution.py
@@ -59,7 +59,7 @@
     is_down = (gy == 0) | (gy == half)
     is_up = (gy == half - 1) | (gy == ny - 1)
     is_next = (gy == half - 2) | (gy == ny - 2)
-    at_end = is_up & (lax.rem(gx, 4) == 3)
+    at_end = is_up & ((lax.rem(gx, 4) == 3) | (gx == 0))
     near = jnp.where(lax.rem(gx, 4) == 0, 2, 1)
 
     sign = jnp.where(is_up, -1, 1)
@@ -166,11 +166,13 @@
         for r, q in directions:
             halo_copy(kind, r, q).start()
 
+    @pl.when(is_up)
+    def _():
+        for direction in ((2, 1), (2, 2), (2, 0), (0, 1), (0, 2), (1, 0)):
+            for kind in range(2):
+                start(kind, (direction,))
+
     for kind in range(2):
-        @pl.when(is_up)
-        def _():
-            start(kind, ((2, 1), (2, 2), (2, 0), (0, 1), (0, 2), (1, 0)))
-
         @pl.when(is_down)
         def _():
             for q in (1, 2, 0):

time: 33.6 us -> 34.3 us (1.021)
  Pallas kernels: 31.4 us -> 32.1 us
    pallas_call x1, Pallas kernels: 31.4 us -> 32.1 us  [body(): pl.pallas_call(functools.partial(kernel, nx, ny), out_shape=(pltpu.VMEM((...]
where the time goes in v7:
time: 34.3 us; the launch traced here: 34.1 us
  Pallas kernels  32.1 us (94%)
  between operations  1.29 us (4%)
  other arithmetic  0.7 us (2%)
    pallas_call x1, Pallas kernels, body(): pl.pallas_call(functools.partial(kernel, nx, ny), out_shape=(pltpu.VMEM((...  32.1 us
    another operation x1, other arithmetic, body(): lax.reduce(parts, (jnp.float32(0), jnp.float32(0)), lambda a, b: (a[0] +...  0.7 us

profile of v7, /device:TPU:1, one launch (start us, length us, event | category | flops | bytes accessed | tf_op | source)
XLA Modules:
  0.0 34.1 jit_solution(7346874718505963193)
XLA Ops:
  1.3 32.1 %layer.1 = (f32[2,128,128]{2,1,0:T(8,128)S(1)}, f32[2,128,128]{2,1,0:T(8,128)S(1)}) custom-call(bf16[1,1,3,128]{3,2,1,0:T(4,128)(2,1)} %pos_hbm.1, bf16[1,1,128,128]{3,2,1,0:T(8,128)(2,1)} %feat_hbm.1, s32[1,1,1,8]{3,2,1,0:T(1,128)} %senders_hbm.1, s32[1,1,1]{2,1,0:T(1,128)S(6)} %copy.10.counts_hbm, f32[2,8,128]{2,1,0:T(8,128)} %rad_hbm.1, ...), custom_call_target="tpu_custom_call" | custom-call | tf_op jit(solution)/shard_map/layer/pallas_call | solution.py:388
  33.4 0.7 %reduce.15 = (bf16[128,128]{1,0:T(8,128)(2,1)}, f32[128,128]{1,0:T(8,128)}) reduce(f32[2,128,128]{2,1,0:T(8,128)S(1)} %get-tuple-element.6, f32[2,128,128]{2,1,0:T(8,128)S(1)} %get-tuple-element.7, f32[]{:T(128)} %constant.0.clone.1, f32[]{:T(128)} %constant.0.clone.1), dimensions={0}, to_apply=%region_0.0 | reduce | flops 32768 | bytes 360456 | tf_op jit(solution)/shard_map/reduce | solution.py:426
